TPU v7x, 32 devices: a whole 2x2x4 slice. The times are simulated.
32 devices in a mesh: space: 8 (over y, x, core), chan: 4 (over z).
Axes of the slice: x: 2, y: 2, z: 4, core: 2. Of those that a mesh axis runs over, the one named last changes fastest.
Arguments:
- feats: bfloat16 [96, 8, 8, 128], P('chan', 'space'), may hold values from -6 to 6
- grads: bfloat16 [96, 8, 8, 128], P('chan', 'space'), may hold values from -6 to 6
- mask: int32 [8, 8, 128], P('space', None, 'chan'), may hold values 0 or 1
- w_first: bfloat16 [27, 96, 96], replicated, may hold values from -0.125 to 0.125
- w_second: bfloat16 [27, 96, 96], replicated, may hold values from -0.125 to 0.125
Outputs:
- grad_feats: bfloat16 [96, 8, 8, 128], P('chan', 'space')
- grad_first: float32 [27, 96, 96], P(None, None, 'chan')
- grad_second: float32 [27, 96, 96], P(None, None, 'chan')
All inputs are finite; a program needn't handle non-finite values. No bound on the sum of `mask` on one device may be relied on, other than what follows from the above.
Results may differ from a plain program's by a relative error of at most 0.02.
Values may be sent and summed in bfloat16 or wider, within the bound.
A program may use at most 64 MiB of HBM per device.

v0:
```python
import jax
import jax.numpy as jnp
from jax import lax
from jax.sharding import PartitionSpec as P

offset_table = [(a, b, c) for a in (-1, 0, 1) for b in (-1, 0, 1) for c in (-1, 0, 1)]


def extended(block, sides, width):
    for axis, dim in sides:
        count = lax.axis_size(axis)
        forward = [(i, i + 1) for i in range(count - 1)]
        backward = [(target, source) for source, target in forward]
        low = lax.ppermute(
            lax.slice_in_dim(block, block.shape[dim] - width, None, axis=dim), axis, forward
        )
        high = lax.ppermute(lax.slice_in_dim(block, 0, width, axis=dim), axis, backward)
        block = jnp.concatenate([low, block, high], axis=dim)
    return block


def rims(stacked):
    widened = extended(stacked, (("space", 2), ("chan", 4)), 1)
    return jnp.pad(widened, ((0, 0), (0, 0), (0, 0), (1, 1), (0, 0)))


def columns(padded, direction):
    channels, xs, ys, zs = padded.shape
    pieces = []
    for a, b, c in offset_table:
        pieces.append(
            padded[
                :,
                1 + direction * a : xs - 1 + direction * a,
                1 + direction * b : ys - 1 + direction * b,
                1 + direction * c : zs - 1 + direction * c,
            ]
        )
    return jnp.concatenate(pieces, 0).reshape(len(offset_table) * channels, -1)


def contract_last(left, right):
    return lax.dot_general(
        left, right, (((1,), (1,)), ((), ())), preferred_element_type=jnp.float32
    )


def body(feats, grads, mask, w_first, w_second):
    taps = w_first.shape[0]
    channels = w_first.shape[1]
    local_x, local_g = (
        lax.all_to_all(feats, "chan", split_axis=3, concat_axis=0, tiled=True),
        lax.all_to_all(grads, "chan", split_axis=3, concat_axis=0, tiled=True),
    )
    x_cells, y_cells, z_cells = (local_x.shape[1], local_x.shape[2], local_x.shape[3])
    voxels = x_cells * y_cells * z_cells
    weight_mask = mask.astype(jnp.float32).reshape(1, voxels)
    masked = local_g * mask.astype(jnp.bfloat16)[None]
    widened = rims(jnp.stack([local_x, masked]))
    cols_x = columns(widened[0], 1)
    cols_g = columns(widened[1], -1)
    pre = (
        jnp.dot(
            w_first.reshape(taps * channels, channels).T, cols_x, preferred_element_type=jnp.float32
        )
        * weight_mask
    )
    sigm = jax.nn.sigmoid(pre)
    active = (pre * sigm).astype(jnp.bfloat16)
    mixer_second = w_second.transpose(1, 0, 2).reshape(channels, taps * channels)
    back = jnp.dot(mixer_second, cols_g, preferred_element_type=jnp.float32)
    slope = sigm * (1.0 + pre * (1.0 - sigm))
    grad_pre = (back * slope * weight_mask).astype(jnp.bfloat16)
    total_cells = voxels * lax.axis_size("space") * lax.axis_size("chan")
    scale = 1.0 / jnp.sqrt(jnp.float32(total_cells))
    part_second = (
        contract_last(active, cols_g).reshape(channels, taps, channels).transpose(1, 0, 2) * scale
    )
    part_first = contract_last(cols_x, grad_pre).reshape(taps, channels, channels) * scale
    padded_h = rims(grad_pre.reshape(1, channels, x_cells, y_cells, z_cells))[0]
    cols_h = columns(padded_h, -1)
    mixer_first = w_first.transpose(1, 0, 2).reshape(channels, taps * channels)
    grad_in = jnp.dot(mixer_first, cols_h, preferred_element_type=jnp.float32) * weight_mask
    grad_in = grad_in.astype(jnp.bfloat16).reshape(channels, x_cells, y_cells, z_cells)
    grad_feats = lax.all_to_all(grad_in, "chan", split_axis=0, concat_axis=3, tiled=True)
    shares = (
        lax.psum_scatter(
            part_first.astype(jnp.bfloat16), "chan", scatter_dimension=2, tiled=True
        ).astype(jnp.float32),
        lax.psum_scatter(
            part_second.astype(jnp.bfloat16), "chan", scatter_dimension=2, tiled=True
        ).astype(jnp.float32),
    )
    grad_first, grad_second = lax.psum((shares[0], shares[1]), "space")
    return (grad_feats, grad_first, grad_second)


def solution(mesh):
    in_specs = (
        P("chan", "space", None, None),
        P("chan", "space", None, None),
        P("space", None, "chan"),
        P(),
        P(),
    )
    out_specs = (P("chan", "space", None, None), P(None, None, "chan"), P(None, None, "chan"))
    return jax.shard_map(body, mesh=mesh, in_specs=in_specs, out_specs=out_specs, check_vma=False)
```

profile of v0, /device:TPU:0, one launch (start us, length us, event | category | flops | bytes accessed | tf_op | source)
XLA Modules:
  0.0 194.1 jit_solution(8408906219484616610)
XLA Ops:
  7.2 1.1 copy.79
  8.2 1.0 reshape.68
  9.2 6.3 %all-to-all-start.1 = ((bf16[4,2,3072]{2,1,0:T(2,128)(2,1)}), bf16[4,2,3072]{2,1,0:T(2,128)(2,1)S(1)}, u32[]{:S(2)}, u32[]{:S(2)}) async-start(bf16[4,2,3072]{2,1,0:T(2,128)(2,1)} %reshape.68), calls=%async_computation.1 | async-start | bytes 98304 | tf_op jit(solution)/shard_map/all_to_all | solution.py:53
  15.5 1.0 copy.76
  16.6 1.0 reshape.70
  17.5 3.7 %all-to-all-done.1 = bf16[4,2,3072]{2,1,0:T(2,128)(2,1)S(1)} async-done(((bf16[4,2,3072]{2,1,0:T(2,128)(2,1)}), bf16[4,2,3072]{2,1,0:T(2,128)(2,1)S(1)}, u32[]{:S(2)}, u32[]{:S(2)}) %all-to-all-start.1) | async-done | bytes 49184 | tf_op jit(solution)/shard_map/all_to_all | solution.py:53
  21.2 3.3 %all-to-all-start = ((bf16[4,2,3072]{2,1,0:T(2,128)(2,1)}), bf16[4,2,3072]{2,1,0:T(2,128)(2,1)S(1)}, u32[]{:S(2)}, u32[]{:S(2)}) async-start(bf16[4,2,3072]{2,1,0:T(2,128)(2,1)} %reshape.70), calls=%async_computation | async-start | bytes 98304 | tf_op jit(solution)/shard_map/all_to_all | solution.py:52
  24.9 0.4 copy.95
  25.9 4.3 %all-to-all-done = bf16[4,2,3072]{2,1,0:T(2,128)(2,1)S(1)} async-done(((bf16[4,2,3072]{2,1,0:T(2,128)(2,1)}), bf16[4,2,3072]{2,1,0:T(2,128)(2,1)S(1)}, u32[]{:S(2)}, u32[]{:S(2)}) %all-to-all-start) | async-done | bytes 49184 | tf_op jit(solution)/shard_map/all_to_all | solution.py:52
  30.5 0.4 copy.94
  31.6 1.3 collective-permute-start
  32.9 1.3 collective-permute-start.1
  34.2 3.7 %collective-permute-done.1 = bf16[2,96,1,8,32]{1,4,3,2,0:T(8,128)(2,1)S(1)} collective-permute-done((bf16[2,96,1,8,32]{1,4,3,2,0:T(8,128)(2,1)S(1)}, bf16[2,96,1,8,32]{1,4,3,2,0:T(8,128)(2,1)S(1)}, u32[]{:S(2)}, u32[]{:S(2)}) %collective-permute-start.1) | collective-permute-done | bytes 98336 | tf_op jit(solution)/shard_map/ppermute | solution.py:17
  37.9 2.7 %collective-permute-start.2 = (bf16[2,96,3,8,1]{1,4,3,2,0:T(2,128)(2,1)S(1)}, bf16[2,96,3,8,1]{1,4,3,2,0:T(2,128)(2,1)S(1)}, u32[]{:S(2)}, u32[]{:S(2)}) collective-permute-start(bf16[2,96,3,8,1]{1,4,3,2,0:T(2,128)(2,1)S(1)} %get-tuple-element.26), channel_id=1, source_target_pairs={{0,1},{1,2},{2,3},{4,5},{5,6},{6,7},{8,9},{9,10},{10,11},{12,13},{... | collective-permute-start | bytes 27656 | tf_op jit(solution)/shard_map/ppermute | solution.py:14
  40.7 1.3 collective-permute-start.3
  42.4 4.0 %collective-permute-done.3 = bf16[2,96,3,8,1]{1,4,3,2,0:T(2,128)(2,1)S(1)} collective-permute-done((bf16[2,96,3,8,1]{1,4,3,2,0:T(2,128)(2,1)S(1)}, bf16[2,96,3,8,1]{1,4,3,2,0:T(2,128)(2,1)S(1)}, u32[]{:S(2)}, u32[]{:S(2)}) %collective-permute-start.3) | collective-permute-done | bytes 9248 | tf_op jit(solution)/shard_map/ppermute | solution.py:17
  46.7 0.9 fusion.45
  47.6 0.8 fusion.46
  48.4 1.0 fusion.47
  49.4 2.6 %concatenate.24 = bf16[2592,1,8,32]{0,3,2,1:T(8,128)(2,1)S(1)} concatenate(bf16[96,1,8,32]{0,3,2,1:T(8,128)(2,1)} %get-tuple-element.81, bf16[96,1,8,32]{0,3,2,1:T(8,128)(2,1)} %get-tuple-element.80, bf16[96,1,8,32]{0,3,2,1:T(8,128)(2,1)} %get-tuple-element.79, bf16[96,1,8,32]{0,3,2,1:T(8,128)(2,1)} %get-tuple-element.78, bf16[96,1,8,32]{0,3,2,1:T(8,128)(2,1)} %get-tuple-element.77, ...), dimensions={0} | concatenate | bytes 2654208 | tf_op jit(solution)/shard_map/concatenate | solution.py:39
  52.1 3.5 %dot_general.25 = bf16[27,96,256]{1,0,2:T(8,128)(2,1)} reshape(bf16[2592,1,8,32]{0,3,2,1:T(8,128)(2,1)S(1)} %concatenate.24) | data formatting | bytes 2654208 | tf_op jit(solution)/shard_map/dot_general | solution.py:43
  55.6 0.6 fusion.20
  56.2 2.7 %concatenate.23 = bf16[2592,1,8,32]{0,3,2,1:T(8,128)(2,1)S(1)} concatenate(bf16[96,1,8,32]{0,3,2,1:T(8,128)(2,1)S(1)} %get-tuple-element.113, bf16[96,1,8,32]{0,3,2,1:T(8,128)(2,1)S(1)} %get-tuple-element.114, bf16[96,1,8,32]{0,3,2,1:T(8,128)(2,1)S(1)} %get-tuple-element.115, bf16[96,1,8,32]{0,3,2,1:T(8,128)(2,1)S(1)} %get-tuple-element.116, ...), dimensions={0} | concatenate | bytes 2654208 | tf_op jit(solution)/shard_map/concatenate | solution.py:39
  58.9 0.6 fusion.23
  59.4 1.0 copy-done.1
  60.4 1.6 fusion.13
  62.2 4.0 %collective-permute-start.4 = (bf16[1,96,1,8,32]{1,4,3,2,0:T(8,128)(2,1)S(1)}, bf16[1,96,1,8,32]{1,4,3,2,0:T(8,128)(2,1)S(1)}, u32[]{:S(2)}, u32[]{:S(2)}) collective-permute-start(bf16[1,96,1,8,32]{1,4,3,2,0:T(8,128)(2,1)S(1)} %bitcast.90), channel_id=1, source_target_pairs={{0,4},{4,8},{8,12},{12,16},{16,20},{20,24},{24,28},{1,5},{5,9},{9,... | collective-permute-start | bytes 147464 | tf_op jit(solution)/shard_map/ppermute | solution.py:14
  66.3 1.3 collective-permute-start.5
  67.9 0.6 dynamic-slice
  69.2 3.5 %dot_general.27 = bf16[27,96,256]{1,0,2:T(8,128)(2,1)} reshape(bf16[2592,1,8,32]{0,3,2,1:T(8,128)(2,1)S(1)} %concatenate.23) | data formatting | bytes 2654208 | tf_op jit(solution)/shard_map/dot_general | solution.py:43
  72.7 2.3 %collective-permute-start.6 = (bf16[1,96,3,8,1]{1,4,3,2,0:T(2,128)(2,1)S(1)}, bf16[1,96,3,8,1]{1,4,3,2,0:T(2,128)(2,1)S(1)}, u32[]{:S(2)}, u32[]{:S(2)}) collective-permute-start(bf16[1,96,3,8,1]{1,4,3,2,0:T(2,128)(2,1)S(1)} %get-tuple-element.109), channel_id=1, source_target_pairs={{0,1},{1,2},{2,3},{4,5},{5,6},{6,7},{8,9},{9,10},{10,11},{12,13},{... | collective-permute-start | bytes 13832 | tf_op jit(solution)/shard_map/ppermute | solution.py:14
  75.1 1.5 collective-permute-start.7
  76.6 2.4 %fusion.16 = bf16[27,96,96]{2,1,0:T(8,128)(2,1)S(1)} fusion(bf16[27,96,256]{1,0,2:T(8,128)(2,1)} %dot_general.27, f32[96,256]{1,0:T(8,128)S(1)} %fusion.20), kind=kOutput, calls=%fused_computation.10 | convolution fusion | flops 128022528 | bytes 1923072 | tf_op jit(solution)/shard_map/dot_general | solution.py:43
  79.0 2.0 %copy.91 = bf16[27,96,96]{1,0,2:T(8,128)(2,1)} copy(bf16[27,96,96]{2,1,0:T(8,128)(2,1)S(1)} %fusion.16) | data formatting | bytes 995328 | tf_op jit(solution)/shard_map/convert_element_type | solution.py:91
  81.2 0.8 fusion.43
  82.0 2.3 %concatenate.27 = bf16[2592,1,8,32]{0,3,2,1:T(8,128)(2,1)S(1)} concatenate(bf16[96,1,8,32]{0,3,2,1:T(8,128)(2,1)S(1)} %get-tuple-element.54, bf16[96,1,8,32]{0,3,2,1:T(8,128)(2,1)S(1)} %get-tuple-element.53, bf16[96,1,8,32]{0,3,2,1:T(8,128)(2,1)S(1)} %get-tuple-element.52, bf16[96,1,8,32]{0,3,2,1:T(8,128)(2,1)S(1)} %get-tuple-element.51, ...), dimensions={0} | concatenate | bytes 2654208 | tf_op jit(solution)/shard_map/concatenate | solution.py:39
  84.4 0.6 fusion.25
  85.2 0.8 reshape.72
  86.1 3.9 %all-to-all-start.2 = ((bf16[4,2,3072]{2,1,0:T(2,128)(2,1)}), bf16[4,2,3072]{2,1,0:T(2,128)(2,1)S(1)}, u32[]{:S(2)}, u32[]{:S(2)}) async-start(bf16[4,2,3072]{2,1,0:T(2,128)(2,1)} %reshape.72), calls=%async_computation.2 | async-start | bytes 98304 | tf_op jit(solution)/shard_map/all_to_all | solution.py:85
  90.0 14.5 %all-reduce.9.cloned.1.call-done = bf16[27,96,96]{1,2,0:T(8,128)(2,1)} async-done(((bf16[27,96,96]{1,2,0:T(8,128)(2,1)}), bf16[27,96,96]{1,2,0:T(8,128)(2,1)}) %all-reduce.9.cloned.1.call-update) | async-done | bytes 497680
  104.5 1.7 dynamic-slice_convert_fusion
  106.6 0.4 copy.88
  107.0 0.8 all_to_all.47
  107.7 21.6 %reduce-scatter.3.cloned.1.call-done = bf16[27,96,24]{1,0,2:T(8,128)(2,1)} async-done(((bf16[27,96,96]{1,0,2:T(8,128)(2,1)}), bf16[27,96,24]{1,0,2:T(8,128)(2,1)}) %reduce-scatter.3.cloned.1.call-update) | async-done | bytes 124432 | tf_op jit(solution)/shard_map/reduce_scatter | solution.py:90
  129.4 28.2 %all-reduce.10 = f32[27,96,24]{1,0,2:T(8,128)S(1)} all-reduce(bf16[27,96,24]{1,0,2:T(8,128)(2,1)} %reduce-scatter.3.cloned.1.call-done), channel_id=1, replica_groups=mesh['space'=8,'chan'=4] {'space'}, use_global_device_ids=true, to_apply=%region_3.4 | all-reduce | flops 62208 | bytes 373248 | tf_op jit(solution)/shard_map/psum | solution.py:94
  157.5 0.9 copy.93
  158.5 27.4 %all-reduce.7.cloned.1.call-done = f32[27,96,24]{1,2,0:T(8,128)} async-done(((f32[27,96,24]{1,2,0:T(8,128)}), f32[27,96,24]{1,2,0:T(8,128)}) %all-reduce.7.cloned.1.call-update) | async-done | bytes 248848 | tf_op jit(solution)/shard_map/psum | solution.py:94
  185.8 1.7 copy.117
  (53 shorter events, 4.1 us)
Async XLA Ops:
  7.2 17.4 %copy-start.7 = (s32[1,8,32]{2,1,0:T(8,128)S(1)}, s32[1,8,32]{2,1,0:T(8,128)}, u32[]{:S(2)}) copy-start(s32[1,8,32]{2,1,0:T(8,128)} %param.7) | copy-start | bytes 3076
  9.2 12.0 %all-to-all-start.1 = ((bf16[4,2,3072]{2,1,0:T(2,128)(2,1)}), bf16[4,2,3072]{2,1,0:T(2,128)(2,1)S(1)}, u32[]{:S(2)}, u32[]{:S(2)}) async-start(bf16[4,2,3072]{2,1,0:T(2,128)(2,1)} %reshape.68), calls=%async_computation.1 | async-start | bytes 98304 | tf_op jit(solution)/shard_map/all_to_all | solution.py:53
  21.2 8.9 %all-to-all-start = ((bf16[4,2,3072]{2,1,0:T(2,128)(2,1)}), bf16[4,2,3072]{2,1,0:T(2,128)(2,1)S(1)}, u32[]{:S(2)}, u32[]{:S(2)}) async-start(bf16[4,2,3072]{2,1,0:T(2,128)(2,1)} %reshape.70), calls=%async_computation | async-start | bytes 98304 | tf_op jit(solution)/shard_map/all_to_all | solution.py:52
  24.5 80.0 %all-reduce.9.cloned.1.call-start = ((), (), s32[]{:S(2)}) async-start(), calls=%async_computation.6 | async-start | bytes 1327104
  25.7 16.4 %copy-start.2 = (bf16[27,96,96]{2,1,0:T(8,128)(2,1)S(1)}, bf16[27,96,96]{2,1,0:T(8,128)(2,1)}, u32[]{:S(2)}) copy-start(bf16[27,96,96]{2,1,0:T(8,128)(2,1)} %param.9) | copy-start | bytes 1492996
  31.6 2.6 %collective-permute-start = (bf16[2,96,1,8,32]{1,4,3,2,0:T(8,128)(2,1)S(1)}, bf16[2,96,1,8,32]{1,4,3,2,0:T(8,128)(2,1)S(1)}, u32[]{:S(2)}, u32[]{:S(2)}) collective-permute-start(bf16[2,96,1,8,32]{1,4,3,2,0:T(8,128)(2,1)S(1)} %pad_maximum_fusion), channel_id=1, source_target_pairs={{0,4},{4,8},{8,12},{12,16},{16,20},{20,24},{24,28},{1,5},{5,9},{9,... | collective-permute-start | bytes 294920 | tf_op jit(solution)/shard_map/ppermute | solution.py:14
  32.9 5.0 %collective-permute-start.1 = (bf16[2,96,1,8,32]{1,4,3,2,0:T(8,128)(2,1)S(1)}, bf16[2,96,1,8,32]{1,4,3,2,0:T(8,128)(2,1)S(1)}, u32[]{:S(2)}, u32[]{:S(2)}) collective-permute-start(bf16[2,96,1,8,32]{1,4,3,2,0:T(8,128)(2,1)S(1)} %pad_maximum_fusion), channel_id=1, source_target_pairs={{4,0},{8,4},{12,8},{16,12},{20,16},{24,20},{28,24},{5,1},{9,5},{13... | collective-permute-start | bytes 294920 | tf_op jit(solution)/shard_map/ppermute | solution.py:17
  37.9 4.5 %collective-permute-start.2 = (bf16[2,96,3,8,1]{1,4,3,2,0:T(2,128)(2,1)S(1)}, bf16[2,96,3,8,1]{1,4,3,2,0:T(2,128)(2,1)S(1)}, u32[]{:S(2)}, u32[]{:S(2)}) collective-permute-start(bf16[2,96,3,8,1]{1,4,3,2,0:T(2,128)(2,1)S(1)} %get-tuple-element.26), channel_id=1, source_target_pairs={{0,1},{1,2},{2,3},{4,5},{5,6},{6,7},{8,9},{9,10},{10,11},{12,13},{... | collective-permute-start | bytes 27656 | tf_op jit(solution)/shard_map/ppermute | solution.py:14
  40.7 5.7 %collective-permute-start.3 = (bf16[2,96,3,8,1]{1,4,3,2,0:T(2,128)(2,1)S(1)}, bf16[2,96,3,8,1]{1,4,3,2,0:T(2,128)(2,1)S(1)}, u32[]{:S(2)}, u32[]{:S(2)}) collective-permute-start(bf16[2,96,3,8,1]{1,4,3,2,0:T(2,128)(2,1)S(1)} %get-tuple-element.27), channel_id=1, source_target_pairs={{1,0},{2,1},{3,2},{5,4},{6,5},{7,6},{9,8},{10,9},{11,10},{13,12},{... | collective-permute-start | bytes 27656 | tf_op jit(solution)/shard_map/ppermute | solution.py:17
  52.1 3.5 %copy-start = (bf16[27,96,96]{2,1,0:T(8,128)(2,1)S(1)}, bf16[27,96,96]{2,1,0:T(8,128)(2,1)}, u32[]{:S(2)}) copy-start(bf16[27,96,96]{2,1,0:T(8,128)(2,1)} %param.8) | copy-start | bytes 1492996
  58.8 1.6 copy-start.1
  62.1 5.9 %copy-start.8 = (u32[32]{0:T(128)S(1)}, u32[32]{0:T(128)}, u32[]{:S(2)}) copy-start(u32[32]{0:T(128)} %constant.16) | copy-start | bytes 388
  62.1 67.3 %reduce-scatter.3.cloned.1.call-start = ((), (), s32[]{:S(2)}) async-start(), calls=%async_computation.5 | async-start | bytes 983040 | tf_op jit(solution)/shard_map/reduce_scatter | solution.py:90
  62.2 10.4 %collective-permute-start.4 = (bf16[1,96,1,8,32]{1,4,3,2,0:T(8,128)(2,1)S(1)}, bf16[1,96,1,8,32]{1,4,3,2,0:T(8,128)(2,1)S(1)}, u32[]{:S(2)}, u32[]{:S(2)}) collective-permute-start(bf16[1,96,1,8,32]{1,4,3,2,0:T(8,128)(2,1)S(1)} %bitcast.90), channel_id=1, source_target_pairs={{0,4},{4,8},{8,12},{12,16},{16,20},{20,24},{24,28},{1,5},{5,9},{9,... | collective-permute-start | bytes 147464 | tf_op jit(solution)/shard_map/ppermute | solution.py:14
  66.3 6.4 %collective-permute-start.5 = (bf16[1,96,1,8,32]{1,4,3,2,0:T(8,128)(2,1)S(1)}, bf16[1,96,1,8,32]{1,4,3,2,0:T(8,128)(2,1)S(1)}, u32[]{:S(2)}, u32[]{:S(2)}) collective-permute-start(bf16[1,96,1,8,32]{1,4,3,2,0:T(8,128)(2,1)S(1)} %bitcast.91), channel_id=1, source_target_pairs={{4,0},{8,4},{12,8},{16,12},{20,16},{24,20},{28,24},{5,1},{9,5},{13... | collective-permute-start | bytes 147464 | tf_op jit(solution)/shard_map/ppermute | solution.py:17
  72.7 2.4 %copy-start.3 = (bf16[1,96,1,8,32]{1,4,3,2,0:T(8,128)(2,1)}, bf16[1,96,1,8,32]{1,4,3,2,0:T(8,128)(2,1)S(1)}, u32[]{:S(2)}) copy-start(bf16[1,96,1,8,32]{1,4,3,2,0:T(8,128)(2,1)S(1)} %collective-permute-done.4) | copy-start | bytes 147460
  72.7 2.4 %copy-start.5 = (bf16[1,96,1,8,32]{1,4,3,2,0:T(8,128)(2,1)}, bf16[1,96,1,8,32]{1,4,3,2,0:T(8,128)(2,1)S(1)}, u32[]{:S(2)}) copy-start(bf16[1,96,1,8,32]{1,4,3,2,0:T(8,128)(2,1)S(1)} %collective-permute-done.5) | copy-start | bytes 147460
  72.7 8.2 %collective-permute-start.6 = (bf16[1,96,3,8,1]{1,4,3,2,0:T(2,128)(2,1)S(1)}, bf16[1,96,3,8,1]{1,4,3,2,0:T(2,128)(2,1)S(1)}, u32[]{:S(2)}, u32[]{:S(2)}) collective-permute-start(bf16[1,96,3,8,1]{1,4,3,2,0:T(2,128)(2,1)S(1)} %get-tuple-element.109), channel_id=1, source_target_pairs={{0,1},{1,2},{2,3},{4,5},{5,6},{6,7},{8,9},{9,10},{10,11},{12,13},{... | collective-permute-start | bytes 13832 | tf_op jit(solution)/shard_map/ppermute | solution.py:14
  75.1 5.9 %collective-permute-start.7 = (bf16[1,96,3,8,1]{1,4,3,2,0:T(2,128)(2,1)S(1)}, bf16[1,96,3,8,1]{1,4,3,2,0:T(2,128)(2,1)S(1)}, u32[]{:S(2)}, u32[]{:S(2)}) collective-permute-start(bf16[1,96,3,8,1]{1,4,3,2,0:T(2,128)(2,1)S(1)} %get-tuple-element.110), channel_id=1, source_target_pairs={{1,0},{2,1},{3,2},{5,4},{6,5},{7,6},{9,8},{10,9},{11,10},{13,12},{... | collective-permute-start | bytes 13832 | tf_op jit(solution)/shard_map/ppermute | solution.py:17
  79.0 2.0 %copy-start.4 = (bf16[1,96,1,8,32]{1,4,3,2,0:T(8,128)(2,1)S(1)}, bf16[1,96,1,8,32]{1,4,3,2,0:T(8,128)(2,1)}, u32[]{:S(2)}) copy-start(bf16[1,96,1,8,32]{1,4,3,2,0:T(8,128)(2,1)} %copy-done.3) | copy-start | bytes 147460
  79.0 2.0 %copy-start.6 = (bf16[1,96,1,8,32]{1,4,3,2,0:T(8,128)(2,1)S(1)}, bf16[1,96,1,8,32]{1,4,3,2,0:T(8,128)(2,1)}, u32[]{:S(2)}) copy-start(bf16[1,96,1,8,32]{1,4,3,2,0:T(8,128)(2,1)} %copy-done.5) | copy-start | bytes 147460
  86.1 20.1 %all-to-all-start.2 = ((bf16[4,2,3072]{2,1,0:T(2,128)(2,1)}), bf16[4,2,3072]{2,1,0:T(2,128)(2,1)S(1)}, u32[]{:S(2)}, u32[]{:S(2)}) async-start(bf16[4,2,3072]{2,1,0:T(2,128)(2,1)} %reshape.72), calls=%async_computation.2 | async-start | bytes 98304 | tf_op jit(solution)/shard_map/all_to_all | solution.py:85
  90.0 95.8 %all-reduce.7.cloned.1.call-start = ((), (), s32[]{:S(2)}) async-start(), calls=%async_computation.4 | async-start | bytes 663552 | tf_op jit(solution)/shard_map/psum | solution.py:94
Sparse Core Ops, SparseCore 0:
  62.2 42.2 all-reduce.8
  106.9 22.4 reduce-scatter.2
  133.4 52.4 all-reduce.6
where the time goes:
time: 195 us; the launch traced here: 194 us
  waiting for transfers between devices  79.1 us (41%)
  local copies, waits for them, and re-layouts  34.7 us (18%)
  starting transfers between devices  29.3 us (15%)
  blocking collectives  28.2 us (14%)
  between operations  14.9 us (8%)
  matrix products  5.68 us (3%)
  other arithmetic  2.25 us (1%)
    psum x1, blocking collectives, body(): grad_first, grad_second = lax.psum((shares[0], shares[1]), 'space')  28.2 us
    psum x1, waiting for transfers between devices, body(): grad_first, grad_second = lax.psum((shares[0], shares[1]), 'space')  27.4 us
    reduce_scatter x1, waiting for transfers between devices, body(): lax.psum_scatter(part_second.astype(jnp.bfloat16), 'chan', scatter_dimens...  21.6 us
    unnamed x4, waiting for transfers between devices  14.5 us
    ppermute x4, starting transfers between devices, extended(): lax.ppermute(lax.slice_in_dim(block, block.shape[dim] - width, None, axis...  10.4 us
    unnamed x29, local copies, waits for them, and re-layouts  10 us
    ppermute x4, waiting for transfers between devices, extended(): lax.ppermute(lax.slice_in_dim(block, 0, width, axis=dim), axis, backward)  7.65 us
    concatenate x3, local copies, waits for them, and re-layouts, columns(): return jnp.concatenate(pieces, 0).reshape(len(offset_table) * channels, -1)  7.64 us
  transfers between devices with their start and end apart: 14, of which 7 were waited for; matrix products, arithmetic and copies ran while one was open for 11% of the time, Pallas kernels for 0%

commit v1 on v0

v1 whole, which is shorter than its diff:
```python
import functools

import jax
import jax.numpy as jnp
from jax import lax
from jax.experimental import pallas as pl
from jax.experimental.pallas import tpu as pltpu
from jax.sharding import PartitionSpec as P

MESH = pl.DeviceIdType.MESH
F32 = jnp.float32
BF16 = jnp.bfloat16


def dot_nn(left, right):
    return jnp.dot(left, right, preferred_element_type=F32)


def dot_nt(left, right):
    return lax.dot_general(left, right, (((1,), (1,)), ((), ())), preferred_element_type=F32)


def one_hot(rows, cols, target):
    r = lax.broadcasted_iota(jnp.int32, (rows, cols), 0)
    q = lax.broadcasted_iota(jnp.int32, (rows, cols), 1)
    return jnp.where(target(r, q), 1.0, 0.0).astype(BF16)


def lane_shift(x, s):
    if s == 0:
        return x
    n = x.shape[1]
    z = lax.broadcasted_iota(jnp.int32, x.shape, 1)
    if s == 1:
        return jnp.where(z < n - 1, pltpu.roll(x, n - 1, 1), 0.0)
    return jnp.where(z > 0, pltpu.roll(x, 1, 1), 0.0)


def tap_sum(p_ref, base, cb, ys, zs, y, direction):
    total = None
    for c in (-1, 0, 1):
        acc = None
        for b in (-1, 0, 1):
            yy = y + direction * b
            if 0 <= yy < ys:
                j = 3 * (b + 1) + (c + 1)
                piece = p_ref[base + j * cb : base + (j + 1) * cb, yy * zs : (yy + 1) * zs]
                acc = piece if acc is None else acc + piece
        acc = lane_shift(acc, direction * c)
        total = acc if total is None else total + acc
    return total


def spread(out_ref, rows_of, cb, ys, zs):
    for y in range(ys):
        row = rows_of(y)
        for c in (-1, 0, 1):
            moved = lane_shift(row, -c)
            for b in (-1, 0, 1):
                j = 3 * (b + 1) + (c + 1)
                if 0 <= y + b < ys:
                    out_ref[j * cb : (j + 1) * cb, (y + b) * zs : (y + b + 1) * zs] = moved
    edge = jnp.zeros((3 * cb, zs), F32)
    out_ref[0 : 3 * cb, (ys - 1) * zs : ys * zs] = edge
    out_ref[6 * cb : 9 * cb, 0:zs] = edge


def kernel(
    n, nz, ys, zs, scale, sp, ch_name,
    block_ref, mask_ref, w1_ref, w2_ref,
    gf_ref, g1_ref, g2_ref,
    B, MK, MX, M, W, WA, WB, WC, WH, PS, SH, SM, C, H, R32, R1, RR1, G1, R2, RR2, G2,
    zs1, zr1, hs1, hr1, ms1, mr1, mhs, mhr, zs2, zr2, hs2, hr2, s1, q1, s2, q2, t1, u1, t2, u2,
):
    s = lax.axis_index(sp)
    me = lax.axis_index(ch_name)
    cb2, cells = block_ref.shape
    cb = cb2 // 2
    full = cb * nz
    hrows = H.shape[2]
    mz = mask_ref.shape[1]
    rows = 27 * cb

    def copy(src, dst, ssem, rsem, ds, dc):
        return pltpu.make_async_remote_copy(
            src_ref=src, dst_ref=dst, send_sem=ssem, recv_sem=rsem,
            device_id=(ds, dc), device_id_type=MESH,
        )

    barrier = pltpu.get_barrier_semaphore()

    @pl.loop(1, nz)
    def _(i):
        pl.semaphore_signal(barrier, inc=1, device_id=(s, lax.rem(me + i, nz)), device_id_type=MESH)

    @pl.loop(1, n)
    def _(i):
        pl.semaphore_signal(barrier, inc=1, device_id=(lax.rem(s + i, n), me), device_id_type=MESH)

    B[1, me] = block_ref[...]
    place = one_hot(mz, zs, lambda r, q: q == r + mz * me)
    MK[me] = dot_nn(mask_ref[...].astype(F32).astype(BF16), place)
    pl.semaphore_wait(barrier, n + nz - 2)

    def z_copy(i, buf, ssem, rsem):
        return copy(buf, buf, ssem.at[i], rsem.at[i], s, lax.rem(me + i, nz))

    order = sorted(range(1, nz), key=lambda i: min(i, nz - i))
    for i in order:
        z_copy(i, MK.at[me], ms1, mr1).start()
    for i in order:
        z_copy(i, B.at[1, me], zs1, zr1).start()

    def halo(c, start):
        src = B.at[1, c]

        @pl.when(s < n - 1)
        def _():
            d = copy(src, B.at[0, c], hs1.at[0, c], hr1.at[0, c], s + 1, me)
            d.start() if start else d.wait_send()

        @pl.when(s > 0)
        def _():
            d = copy(src, B.at[2, c], hs1.at[1, c], hr1.at[1, c], s - 1, me)
            d.start() if start else d.wait_send()

    halo(me, True)

    pick = one_hot(cb, full, lambda r, q: q == r + cb * me)

    @pl.loop(0, 27)
    def _(k):
        w1 = w1_ref[k]
        W[0, k] = dot_nt(pick, w1)
        W[1, k] = dot_nn(pick, w2_ref[k])
        W[2, k] = dot_nn(pick, w1)

    to_first = one_hot(full, nz * cb2, lambda r, q: q == (r // cb) * cb2 + lax.rem(r, cb))
    to_second = one_hot(full, nz * cb2, lambda r, q: q == (r // cb) * cb2 + cb + lax.rem(r, cb))
    to_halo = one_hot(full, nz * hrows, lambda r, q: q == (r // cb) * hrows + lax.rem(r, cb))
    for a in range(3):
        part = W[0, 9 * a : 9 * a + 9].reshape(9 * cb, full).astype(BF16)
        WA[a] = dot_nn(part, to_first).astype(BF16)
        part = W[1, 9 * a : 9 * a + 9].reshape(9 * cb, full).astype(BF16)
        WB[a] = dot_nn(part, to_second).astype(BF16)
    for a in range(3):
        part = W[2, 9 * a : 9 * a + 9].reshape(9 * cb, full).astype(BF16)
        if a == 1:
            WC[...] = dot_nn(part, to_first).astype(BF16)
        else:
            WH[a // 2] = dot_nn(part, to_halo).astype(BF16)

    for i in order:
        c = lax.rem(me + nz - i, nz)
        copy(MK.at[c], MK.at[c], ms1.at[i], mr1.at[i], s, c).wait_recv()
    own_mask = MK[0]
    for c in range(1, nz):
        own_mask = own_mask + MK[c]
    MX[1] = own_mask

    @pl.when(s < n - 1)
    def _():
        copy(MX.at[1], MX.at[0], mhs.at[0], mhr.at[0], s + 1, me).start()

    @pl.when(s > 0)
    def _():
        copy(MX.at[1], MX.at[2], mhs.at[1], mhr.at[1], s - 1, me).start()

    for i in order:
        c = lax.rem(me + nz - i, nz)
        copy(B.at[1, c], B.at[1, c], zs1.at[i], zr1.at[i], s, c).wait_recv()
        halo(c, True)

    is_grad = lax.rem(lax.broadcasted_iota(jnp.int32, (nz * cb2, zs), 0), cb2) >= cb

    def apply_mask(slab):
        for y in range(ys):
            piece = B[slab, :, :, y * zs : (y + 1) * zs].reshape(nz * cb2, zs)
            factor = jnp.where(is_grad, MX[slab, y : y + 1, :], 1.0).astype(BF16)
            M[slab, :, y * zs : (y + 1) * zs] = piece * factor

    def multiply(slab, first):
        a1, a2 = slab, 2 - slab
        x = M[slab]
        if first:
            PS[0] = dot_nn(WA[a1], x)
            PS[1] = dot_nn(WB[a2], x)
        else:
            PS[0] += dot_nn(WA[a1], x)
            PS[1] += dot_nn(WB[a2], x)

    def spread_masked(slab):
        own = B[slab, me].astype(F32)[cb:cb2]
        spread(
            SM.at[2 - slab],
            lambda y: own[:, y * zs : (y + 1) * zs] * MX[slab, y : y + 1, :],
            cb, ys, zs,
        )

    apply_mask(1)
    multiply(1, True)
    spread_masked(1)
    for side, slab, there in ((0, 0, s > 0), (1, 2, s < n - 1)):

        @pl.when(there)
        def _():
            copy(MX.at[slab], MX.at[slab], mhs.at[side], mhr.at[side], s, me).wait_recv()

            @pl.loop(0, nz)
            def _(c):
                copy(B.at[slab, c], B.at[slab, c], hs1.at[side, c], hr1.at[side, c], s, me).wait_recv()

            apply_mask(slab)
            spread_masked(slab)
            multiply(slab, False)

        @pl.when(jnp.logical_not(there))
        def _():
            M[slab] = jnp.zeros(M.shape[1:], BF16)
            SM[2 - slab] = jnp.zeros(SM.shape[1:], F32)

    for y in range(ys):
        at = slice(y * zs, (y + 1) * zs)
        m = MX[1, y : y + 1, :]
        pre = tap_sum(PS.at[0], 0, cb, ys, zs, y, 1) * m
        back = tap_sum(PS.at[1], 0, cb, ys, zs, y, -1)
        sig = jax.nn.sigmoid(pre)
        active = pre * sig
        slope = sig * (1.0 + pre * (1.0 - sig))
        grad_pre = back * slope * m
        C[me, :, at] = jnp.concatenate([grad_pre, active], axis=0).astype(BF16)

    for i in order:
        z_copy(i, C.at[me], zs2, zr2).start()

    def halo2(c, start):
        src = C.at[c, 0:hrows]

        @pl.when(s < n - 1)
        def _():
            d = copy(src, H.at[0, c], hs2.at[0, c], hr2.at[0, c], s + 1, me)
            d.start() if start else d.wait_send()

        @pl.when(s > 0)
        def _():
            d = copy(src, H.at[1, c], hs2.at[1, c], hr2.at[1, c], s - 1, me)
            d.start() if start else d.wait_send()

    halo2(me, True)

    def scatter(R, RR, ssem, rsem):
        @pl.loop(1, n)
        def _(i):
            p = lax.rem(s + i, n)
            copy(R.at[p], RR.at[i], ssem.at[i], rsem.at[i], p, me).start()

    tail = R32.shape[0] - rows
    if tail:
        R32[rows:, :] = jnp.zeros((tail, full), F32)

    own_gp = C[me].astype(F32)[0:cb]
    spread(SH, lambda y: own_gp[:, y * zs : (y + 1) * zs], cb, ys, zs)
    moved = SH[...].astype(BF16)
    for a in range(3):
        wide = (dot_nt(moved, M[a]) * scale).astype(BF16)
        R32[9 * cb * a : 9 * cb * (a + 1), :] = dot_nt(wide, to_first)
    R1[...] = R32[...].astype(BF16).reshape(R1.shape)
    scatter(R1, RR1, s1, q1)

    for i in order:
        c = lax.rem(me + nz - i, nz)
        copy(C.at[c], C.at[c], zs2.at[i], zr2.at[i], s, c).wait_recv()
        halo2(c, True)

    gathered = C[...].reshape(nz * cb2, cells)
    for a in range(3):
        wide = (dot_nt(SM[a].astype(BF16), gathered) * scale).astype(BF16)
        R32[9 * cb * a : 9 * cb * (a + 1), :] = dot_nt(wide, to_second)
    R2[...] = R32[...].astype(BF16).reshape(R2.shape)
    scatter(R2, RR2, s2, q2)

    PS[0] = dot_nn(WC[...], gathered)

    def gather(R, RR, G, ssem, rsem, ts, us):
        @pl.loop(1, n)
        def _(i):
            copy(RR.at[i], RR.at[i], ssem.at[i], rsem.at[i], s, me).wait_recv()

        total = R[s].astype(F32)
        for i in range(1, n):
            total = total + RR[i].astype(F32)
        G[s] = total.astype(BF16)

        @pl.loop(1, n)
        def _(i):
            p = lax.rem(s + i, n)
            copy(G.at[s], G.at[s], ts.at[i], us.at[i], p, me).start()

    gather(R1, RR1, G1, s1, q1, t1, u1)

    for side, there in ((0, s > 0), (1, s < n - 1)):

        @pl.when(there)
        def _():
            @pl.loop(0, nz)
            def _(c):
                copy(H.at[side, c], H.at[side, c], hs2.at[side, c], hr2.at[side, c], s, me).wait_recv()

            PS[0] += dot_nn(WH[1 - side], H[side].reshape(nz * hrows, cells))

    gather(R2, RR2, G2, s2, q2, t2, u2)
    for y in range(ys):
        at = slice(y * zs, (y + 1) * zs)
        grad_in = tap_sum(PS.at[0], 0, cb, ys, zs, y, -1) * MX[1, y : y + 1, :]
        gf_ref[:, at] = grad_in.astype(BF16)

    def finish(G, out_ref, ts, us):
        @pl.loop(1, n)
        def _(i):
            p = lax.rem(s + n - i, n)
            copy(G.at[p], G.at[p], ts.at[i], us.at[i], s, me).wait_recv()

        out_ref[...] = G[...].astype(F32).reshape(R32.shape)[0:rows]

    finish(G1, g1_ref, t1, u1)
    finish(G2, g2_ref, t2, u2)

    for i in order:
        z_copy(i, MK.at[me], ms1, mr1).wait_send()
        z_copy(i, B.at[1, me], zs1, zr1).wait_send()
        z_copy(i, C.at[me], zs2, zr2).wait_send()

    @pl.when(s < n - 1)
    def _():
        copy(MX.at[1], MX.at[0], mhs.at[0], mhr.at[0], s + 1, me).wait_send()

    @pl.when(s > 0)
    def _():
        copy(MX.at[1], MX.at[2], mhs.at[1], mhr.at[1], s - 1, me).wait_send()

    @pl.loop(0, nz)
    def _(c):
        halo(c, False)
        halo2(c, False)

    @pl.loop(1, n)
    def _(i):
        p = lax.rem(s + i, n)
        copy(R1.at[p], RR1.at[i], s1.at[i], q1.at[i], p, me).wait_send()
        copy(R2.at[p], RR2.at[i], s2.at[i], q2.at[i], p, me).wait_send()
        copy(G1.at[s], G1.at[s], t1.at[i], u1.at[i], p, me).wait_send()
        copy(G2.at[s], G2.at[s], t2.at[i], u2.at[i], p, me).wait_send()


def up(value, step):
    return -(-value // step) * step


def body(n, nz, feats, grads, mask, w_first, w_second):
    cb, _, ys, zs = feats.shape
    taps, full, _ = w_first.shape
    cells = ys * zs
    cb2 = 2 * cb
    hrows = up(cb, 16)
    block = jnp.concatenate([feats.reshape(cb, cells), grads.reshape(cb, cells)], axis=0)
    scale = float((n * ys * zs) ** -0.5)
    rows = taps * cb
    piece = up(-(-rows // n), 16)
    vm = pltpu.VMEM
    dma = pltpu.SemaphoreType.DMA
    spec = pl.BlockSpec(memory_space=pltpu.VMEM)
    reduce_bufs = [vm((n, piece, full), BF16)] * 3
    gf, g1, g2 = pl.pallas_call(
        functools.partial(kernel, n, nz, ys, zs, scale, "space", "chan"),
        out_shape=(
            jax.ShapeDtypeStruct((cb, cells), BF16),
            jax.ShapeDtypeStruct((rows, full), F32),
            jax.ShapeDtypeStruct((rows, full), F32),
        ),
        in_specs=[spec] * 4,
        out_specs=(spec,) * 3,
        scratch_shapes=[
            vm((3, nz, cb2, cells), BF16),
            vm((nz, ys, zs), F32),
            vm((3, ys, zs), F32),
            vm((3, nz * cb2, cells), BF16),
            vm((3, taps, cb, full), F32),
            vm((3, 9 * cb, nz * cb2), BF16),
            vm((3, 9 * cb, nz * cb2), BF16),
            vm((9 * cb, nz * cb2), BF16),
            vm((2, 9 * cb, nz * hrows), BF16),
            vm((2, 9 * cb, cells), F32),
            vm((9 * cb, cells), F32),
            vm((3, 9 * cb, cells), F32),
            vm((nz, cb2, cells), BF16),
            vm((2, nz, hrows, cells), BF16),
            vm((n * piece, full), F32),
            *reduce_bufs,
            *reduce_bufs,
            dma((nz,)), dma((nz,)), dma((2, nz)), dma((2, nz)),
            dma((nz,)), dma((nz,)), dma((2,)), dma((2,)),
            dma((nz,)), dma((nz,)), dma((2, nz)), dma((2, nz)),
            dma((n,)), dma((n,)), dma((n,)), dma((n,)),
            dma((n,)), dma((n,)), dma((n,)), dma((n,)),
        ],
        compiler_params=pltpu.CompilerParams(
            collective_id=0, has_side_effects=True, vmem_limit_bytes=48 << 20
        ),
    )(block, mask.reshape(ys, -1), w_first, w_second)
    return (
        gf.reshape(cb, 1, ys, zs),
        g1.reshape(taps, cb, full).transpose(0, 2, 1),
        g2.reshape(taps, cb, full).transpose(0, 2, 1),
    )


def solution(mesh):
    in_specs = (
        P("chan", "space", None, None),
        P("chan", "space", None, None),
        P("space", None, "chan"),
        P(),
        P(),
    )
    out_specs = (P("chan", "space", None, None), P(None, None, "chan"), P(None, None, "chan"))
    sizes = (mesh.shape["space"], mesh.shape["chan"])
    return jax.shard_map(
        functools.partial(body, *sizes),
        mesh=mesh, in_specs=in_specs, out_specs=out_specs, check_vma=False,
    )
```

time: 195 us -> 45.9 us (0.24)
  waiting for transfers between devices: 79.1 us -> 0 us
  Pallas kernels: 0 us -> 39.2 us
  starting transfers between devices: 29.3 us -> 0 us
  local copies, waits for them, and re-layouts: 34.7 us -> 5.76 us
  blocking collectives: 28.2 us -> 0 us
  between operations: 14.9 us -> 0.66 us
  matrix products: 5.68 us -> 0 us
  other arithmetic: 2.25 us -> 0.01 us
    pallas_call x0 -> x1, Pallas kernels: none -> 39.2 us  [body(): pl.pallas_call(functools.partial(kernel, n, nz, ys, zs, scale, 'space', '...]
    psum x1 -> x0, blocking collectives: 28.2 us -> none  [body(): grad_first, grad_second = lax.psum((shares[0], shares[1]), 'space')]
    psum x1 -> x0, waiting for transfers between devices: 27.4 us -> none  [body(): grad_first, grad_second = lax.psum((shares[0], shares[1]), 'space')]
    reduce_scatter x1 -> x0, waiting for transfers between devices: 21.6 us -> none  [body(): lax.psum_scatter(part_second.astype(jnp.bfloat16), 'chan', scatter_dimens...]
    ppermute x8 -> x0, starting transfers between devices: 15.7 us -> none  [the longest x4 10.4 us: extended(): lax.ppermute(lax.slice_in_dim(block, block.shape[dim] - width, None, axis...]
    unnamed x4 -> x0, waiting for transfers between devices: 14.5 us -> none
    all_to_all x3 -> x0, starting transfers between devices: 13.5 us -> none  [the longest x1 6.32 us: body(): lax.all_to_all(grads, 'chan', split_axis=3, concat_axis=0, tiled=True)]
    all_to_all x3 -> x0, waiting for transfers between devices: 7.97 us -> none  [the longest x1 4.28 us: body(): lax.all_to_all(feats, 'chan', split_axis=3, concat_axis=0, tiled=True)]
  transfers between devices with their start and end apart: 14 -> 0, of which waited for: 7 -> 0; matrix products, arithmetic and copies ran while one was open for 11% -> 0% of each run, Pallas kernels for 0% -> 0%
where the time goes in v1:
time: 45.9 us; the launch traced here: 45.6 us
  Pallas kernels  39.2 us (85%)
  local copies, waits for them, and re-layouts  5.76 us (13%)
  between operations  0.66 us (1%)
    pallas_call x1, Pallas kernels, body(): pl.pallas_call(functools.partial(kernel, n, nz, ys, zs, scale, 'space', '...  39.2 us
    unnamed x9, local copies, waits for them, and re-layouts  4.92 us

profile of v1, /device:TPU:0, one launch (start us, length us, event | category | flops | bytes accessed | tf_op | source)
XLA Modules:
  0.0 45.6 jit_solution(12906272741082377861)
XLA Ops:
  0.6 0.8 %copy_bitcast_fusion = (bf16[24,1024]{1,0:T(8,128)(2,1)S(1)}, bf16[24,1024]{1,0:T(8,128)(2,1)S(1)}) fusion(bf16[3,8,8,128]{3,2,1,0:T(8,128)(2,1)} %bitcast.26, bf16[3,8,8,128]{3,2,1,0:T(8,128)(2,1)} %bitcast.27), kind=kLoop, calls=%fused_computation.1 | loop fusion | bytes 196608 | tf_op jit(solution)/shard_map/reshape | solution.py:365
  1.5 0.0 copy-start.2
  1.5 0.7 %copy-done.2 = s32[1,8,32]{2,1,0:T(8,128)S(1)} copy-done((s32[1,8,32]{2,1,0:T(8,128)S(1)}, s32[1,8,32]{2,1,0:T(8,128)}, u32[]{:S(2)}) %copy-start.2) | copy-done | bytes 1048
  2.2 0.0 copy-start
  2.2 1.1 %copy-done = bf16[27,96,96]{2,1,0:T(8,128)(2,1)S(1)} copy-done((bf16[27,96,96]{2,1,0:T(8,128)(2,1)S(1)}, bf16[27,96,96]{2,1,0:T(8,128)(2,1)}, u32[]{:S(2)}) %copy-start) | copy-done | bytes 497688
  3.2 0.0 copy-start.1
  3.3 1.1 %copy-done.1 = bf16[27,96,96]{2,1,0:T(8,128)(2,1)S(1)} copy-done((bf16[27,96,96]{2,1,0:T(8,128)(2,1)S(1)}, bf16[27,96,96]{2,1,0:T(8,128)(2,1)}, u32[]{:S(2)}) %copy-start.1) | copy-done | bytes 497688
  4.3 39.2 %shard_map.76 = (bf16[24,1024]{1,0:T(8,128)(2,1)S(1)}, f32[648,96]{1,0:T(8,128)S(1)}, f32[648,96]{1,0:T(8,128)S(1)}) custom-call(bf16[48,1024]{1,0:T(8,128)(2,1)S(1)} %pad_maximum_fusion.block_ref, s32[8,32]{1,0:T(8,128)S(1)} %bitcast.24, bf16[27,96,96]{2,1,0:T(8,128)(2,1)S(1)} %copy-done, bf16[27,96,96]{2,1,0:T(8,128)(2,1)S(1)} %copy-done.1), custom_call_target="tpu_custom_call" | custom-call | tf_op jit(solution)/shard_map/pallas_call | solution.py:373
  43.5 0.6 %copy.11 = bf16[3,8,8,128]{3,2,1,0:T(8,128)(2,1)} copy(bf16[3,8,8,128]{3,1,2,0:T(8,128)(2,1)S(1)} %bitcast.23) | data formatting | bytes 98304
  44.1 0.7 %copy.16 = f32[27,96,24]{1,2,0:T(8,128)} copy(f32[27,96,24]{1,2,0:T(8,128)S(1)} %bitcast.22) | data formatting | bytes 497664
  44.9 0.7 %copy.17 = f32[27,96,24]{1,2,0:T(8,128)} copy(f32[27,96,24]{1,2,0:T(8,128)S(1)} %bitcast.21) | data formatting | bytes 497664
  (1 shorter events, 0.0 us)
Async XLA Ops:
  1.5 0.7 %copy-start.2 = (s32[1,8,32]{2,1,0:T(8,128)S(1)}, s32[1,8,32]{2,1,0:T(8,128)}, u32[]{:S(2)}) copy-start(s32[1,8,32]{2,1,0:T(8,128)} %param.7) | copy-start | bytes 3076
  2.2 1.1 %copy-start = (bf16[27,96,96]{2,1,0:T(8,128)(2,1)S(1)}, bf16[27,96,96]{2,1,0:T(8,128)(2,1)}, u32[]{:S(2)}) copy-start(bf16[27,96,96]{2,1,0:T(8,128)(2,1)} %w1_ref.1) | copy-start | bytes 1492996
  3.2 1.1 %copy-start.1 = (bf16[27,96,96]{2,1,0:T(8,128)(2,1)S(1)}, bf16[27,96,96]{2,1,0:T(8,128)(2,1)}, u32[]{:S(2)}) copy-start(bf16[27,96,96]{2,1,0:T(8,128)(2,1)} %w2_ref.1) | copy-start | bytes 1492996

commit v2 on v1

--- a/solution.py
+++ b/solution.py
@@ -67,18 +67,20 @@
 
 def kernel(
     n, nz, ys, zs, scale, sp, ch_name,
-    block_ref, mask_ref, w1_ref, w2_ref,
+    feats_hbm, grads_hbm, mask_hbm, w1_hbm, w2_hbm,
     gf_ref, g1_ref, g2_ref,
-    B, MK, MX, M, W, WA, WB, WC, WH, PS, SH, SM, C, H, R32, R1, RR1, G1, R2, RR2, G2,
-    zs1, zr1, hs1, hr1, ms1, mr1, mhs, mhr, zs2, zr2, hs2, hr2, s1, q1, s2, q2, t1, u1, t2, u2,
+    FI, mask_ref, w1_ref, w2_ref, FX, B, MK, MX, M, W, WA, WB, WH, PS, SH, SM, C, H, R32, R1, RR1, G1, R2, RR2, G2,
+    ins, zs1, zf1, zr1, hs1, hr1, ms1, mr1, mhs, mhr, zs2, zf2, zr2, zs3, zf3, zr3, hs2, hr2, s1, q1, s2, q2, t1, u1, t2, u2,
 ):
     s = lax.axis_index(sp)
     me = lax.axis_index(ch_name)
-    cb2, cells = block_ref.shape
-    cb = cb2 // 2
+    cb = FI.shape[1]
+    cb2 = 2 * cb
+    cells = ys * zs
     full = cb * nz
     hrows = H.shape[2]
-    mz = mask_ref.shape[1]
+    mz = mask_ref.shape[2]
+    skip = cb2 - hrows
     rows = 27 * cb
 
     def copy(src, dst, ssem, rsem, ds, dc):
@@ -97,9 +99,25 @@
     def _(i):
         pl.semaphore_signal(barrier, inc=1, device_id=(lax.rem(s + i, n), me), device_id_type=MESH)
 
-    B[1, me] = block_ref[...]
+    loads = [
+        pltpu.make_async_copy(src, dst, ins.at[i])
+        for i, (src, dst) in enumerate((
+            (mask_hbm, mask_ref), (feats_hbm, FI.at[0]), (grads_hbm, FI.at[1]),
+            (w1_hbm, w1_ref), (w2_hbm, w2_ref),
+        ))
+    ]
+    for load in loads:
+        load.start()
+    for load in loads[:3]:
+        load.wait()
+
+    FX[...] = FI[...].astype(F32).reshape(FX.shape)
+    for y in range(ys):
+        B[1, me, :, y * zs : (y + 1) * zs] = jnp.concatenate(
+            [FX[0, :, y, :], FX[1, :, y, :]], axis=0
+        ).astype(BF16)
     place = one_hot(mz, zs, lambda r, q: q == r + mz * me)
-    MK[me] = dot_nn(mask_ref[...].astype(F32).astype(BF16), place)
+    MK[me] = dot_nn(mask_ref[0].astype(F32).astype(BF16), place)
     pl.semaphore_wait(barrier, n + nz - 2)
 
     def z_copy(i, buf, ssem, rsem):
@@ -108,8 +126,50 @@
     order = sorted(range(1, nz), key=lambda i: min(i, nz - i))
     for i in order:
         z_copy(i, MK.at[me], ms1, mr1).start()
-    for i in order:
-        z_copy(i, B.at[1, me], zs1, zr1).start()
+
+    def inside(c):
+        return jnp.logical_and(c >= 0, c < nz)
+
+    def z_own(view, ssem, rsem, start):
+        def go(d, there):
+            @pl.when(there)
+            def _():
+                x = copy(view(me), view(me), ssem.at[d + 2], rsem.at[me], s, me + d)
+                x.start() if start else x.wait_send()
+
+        relayed = [inside(me + 3 * sign) for sign in (1, -1)]
+        for sign in (1, -1):
+            if nz > 3:
+                go(2 * sign, relayed[sign < 0])
+        for sign in (1, -1):
+            go(sign, inside(me + sign))
+        for sign in (1, -1):
+            if nz > 2:
+                go(2 * sign, jnp.logical_and(inside(me + 2 * sign), jnp.logical_not(relayed[sign < 0])))
+
+    def z_rest(view, fsem, rsem, after):
+        for e in range(1, nz):
+            for sign in (1, -1):
+                c = me - sign * e
+
+                @pl.when(inside(c))
+                def _():
+                    if after is not None:
+                        copy(view(c), view(c), fsem.at[c], rsem.at[c], s, me).wait_recv()
+                    if e >= 2:
+
+                        @pl.when(inside(me + sign))
+                        def _():
+                            x = copy(view(c), view(c), fsem.at[c], rsem.at[c], s, me + sign)
+                            x.start() if after is not None else x.wait_send()
+
+                    if after is not None:
+                        after(c)
+
+    def view1(c):
+        return B.at[1, c]
+
+    z_own(view1, zs1, zr1, True)
 
     def halo(c, start):
         src = B.at[1, c]
@@ -126,6 +186,8 @@
 
     halo(me, True)
 
+    for load in loads[3:]:
+        load.wait()
     pick = one_hot(cb, full, lambda r, q: q == r + cb * me)
 
     @pl.loop(0, 27)
@@ -137,7 +199,8 @@
 
     to_first = one_hot(full, nz * cb2, lambda r, q: q == (r // cb) * cb2 + lax.rem(r, cb))
     to_second = one_hot(full, nz * cb2, lambda r, q: q == (r // cb) * cb2 + cb + lax.rem(r, cb))
-    to_halo = one_hot(full, nz * hrows, lambda r, q: q == (r // cb) * hrows + lax.rem(r, cb))
+    to_halo = one_hot(full, nz * hrows, lambda r, q: q == (r // cb) * hrows + (hrows - cb) + lax.rem(r, cb))
+    to_active = one_hot(full, nz * hrows, lambda r, q: q == (r // cb) * hrows + lax.rem(r, cb))
     for a in range(3):
         part = W[0, 9 * a : 9 * a + 9].reshape(9 * cb, full).astype(BF16)
         WA[a] = dot_nn(part, to_first).astype(BF16)
@@ -145,10 +208,7 @@
         WB[a] = dot_nn(part, to_second).astype(BF16)
     for a in range(3):
         part = W[2, 9 * a : 9 * a + 9].reshape(9 * cb, full).astype(BF16)
-        if a == 1:
-            WC[...] = dot_nn(part, to_first).astype(BF16)
-        else:
-            WH[a // 2] = dot_nn(part, to_halo).astype(BF16)
+        WH[a] = dot_nn(part, to_halo).astype(BF16)
 
     for i in order:
         c = lax.rem(me + nz - i, nz)
@@ -166,10 +226,7 @@
     def _():
         copy(MX.at[1], MX.at[2], mhs.at[1], mhr.at[1], s - 1, me).start()
 
-    for i in order:
-        c = lax.rem(me + nz - i, nz)
-        copy(B.at[1, c], B.at[1, c], zs1.at[i], zr1.at[i], s, c).wait_recv()
-        halo(c, True)
+    z_rest(view1, zf1, zr1, lambda c: halo(c, True))
 
     is_grad = lax.rem(lax.broadcasted_iota(jnp.int32, (nz * cb2, zs), 0), cb2) >= cb
 
@@ -228,13 +285,20 @@
         active = pre * sig
         slope = sig * (1.0 + pre * (1.0 - sig))
         grad_pre = back * slope * m
-        C[me, :, at] = jnp.concatenate([grad_pre, active], axis=0).astype(BF16)
-
-    for i in order:
-        z_copy(i, C.at[me], zs2, zr2).start()
+        C[me, :, at] = jnp.concatenate([active, grad_pre], axis=0).astype(BF16)
+
+    def view2(c):
+        return C.at[c, 0:hrows]
+
+    def view3(c):
+        return C.at[c, hrows:cb2]
+
+    z_own(view2, zs2, zr2, True)
+    if skip:
+        z_own(view3, zs3, zr3, True)
 
     def halo2(c, start):
-        src = C.at[c, 0:hrows]
+        src = C.at[c, skip:cb2]
 
         @pl.when(s < n - 1)
         def _():
@@ -258,7 +322,7 @@
     if tail:
         R32[rows:, :] = jnp.zeros((tail, full), F32)
 
-    own_gp = C[me].astype(F32)[0:cb]
+    own_gp = C[me].astype(F32)[cb:cb2]
     spread(SH, lambda y: own_gp[:, y * zs : (y + 1) * zs], cb, ys, zs)
     moved = SH[...].astype(BF16)
     for a in range(3):
@@ -267,19 +331,21 @@
     R1[...] = R32[...].astype(BF16).reshape(R1.shape)
     scatter(R1, RR1, s1, q1)
 
-    for i in order:
-        c = lax.rem(me + nz - i, nz)
-        copy(C.at[c], C.at[c], zs2.at[i], zr2.at[i], s, c).wait_recv()
-        halo2(c, True)
-
-    gathered = C[...].reshape(nz * cb2, cells)
+    def nothing(c):
+        pass
+
+    z_rest(view2, zf2, zr2, nothing if skip else (lambda c: halo2(c, True)))
+
+    gathered = C[:, 0:hrows, :].reshape(nz * hrows, cells)
     for a in range(3):
         wide = (dot_nt(SM[a].astype(BF16), gathered) * scale).astype(BF16)
-        R32[9 * cb * a : 9 * cb * (a + 1), :] = dot_nt(wide, to_second)
+        R32[9 * cb * a : 9 * cb * (a + 1), :] = dot_nt(wide, to_active)
     R2[...] = R32[...].astype(BF16).reshape(R2.shape)
     scatter(R2, RR2, s2, q2)
 
-    PS[0] = dot_nn(WC[...], gathered)
+    if skip:
+        z_rest(view3, zf3, zr3, lambda c: halo2(c, True))
+    PS[0] = dot_nn(WH[1], C[:, skip:cb2, :].reshape(nz * hrows, cells))
 
     def gather(R, RR, G, ssem, rsem, ts, us):
         @pl.loop(1, n)
@@ -306,13 +372,14 @@
             def _(c):
                 copy(H.at[side, c], H.at[side, c], hs2.at[side, c], hr2.at[side, c], s, me).wait_recv()
 
-            PS[0] += dot_nn(WH[1 - side], H[side].reshape(nz * hrows, cells))
+            PS[0] += dot_nn(WH[2 - 2 * side], H[side].reshape(nz * hrows, cells))
 
     gather(R2, RR2, G2, s2, q2, t2, u2)
     for y in range(ys):
         at = slice(y * zs, (y + 1) * zs)
         grad_in = tap_sum(PS.at[0], 0, cb, ys, zs, y, -1) * MX[1, y : y + 1, :]
-        gf_ref[:, at] = grad_in.astype(BF16)
+        FX[0, :, y, :] = grad_in
+    gf_ref[...] = FX[0].astype(BF16).reshape(gf_ref.shape)
 
     def finish(G, out_ref, ts, us):
         @pl.loop(1, n)
@@ -325,10 +392,15 @@
     finish(G1, g1_ref, t1, u1)
     finish(G2, g2_ref, t2, u2)
 
+    z_own(view1, zs1, zr1, False)
+    z_rest(view1, zf1, zr1, None)
+    z_own(view2, zs2, zr2, False)
+    z_rest(view2, zf2, zr2, None)
+    if skip:
+        z_own(view3, zs3, zr3, False)
+        z_rest(view3, zf3, zr3, None)
     for i in order:
         z_copy(i, MK.at[me], ms1, mr1).wait_send()
-        z_copy(i, B.at[1, me], zs1, zr1).wait_send()
-        z_copy(i, C.at[me], zs2, zr2).wait_send()
 
     @pl.when(s < n - 1)
     def _():
@@ -362,7 +434,6 @@
     cells = ys * zs
     cb2 = 2 * cb
     hrows = up(cb, 16)
-    block = jnp.concatenate([feats.reshape(cb, cells), grads.reshape(cb, cells)], axis=0)
     scale = float((n * ys * zs) ** -0.5)
     rows = taps * cb
     piece = up(-(-rows // n), 16)
@@ -373,13 +444,18 @@
     gf, g1, g2 = pl.pallas_call(
         functools.partial(kernel, n, nz, ys, zs, scale, "space", "chan"),
         out_shape=(
-            jax.ShapeDtypeStruct((cb, cells), BF16),
+            jax.ShapeDtypeStruct((cb, 1, ys, zs), BF16),
             jax.ShapeDtypeStruct((rows, full), F32),
             jax.ShapeDtypeStruct((rows, full), F32),
         ),
-        in_specs=[spec] * 4,
+        in_specs=[pl.BlockSpec(memory_space=pltpu.HBM)] * 5,
         out_specs=(spec,) * 3,
         scratch_shapes=[
+            vm((2, cb, 1, ys, zs), BF16),
+            vm((1, ys, mask.shape[2]), jnp.int32),
+            vm((taps, full, full), BF16),
+            vm((taps, full, full), BF16),
+            vm((2, cb, ys, zs), F32),
             vm((3, nz, cb2, cells), BF16),
             vm((nz, ys, zs), F32),
             vm((3, ys, zs), F32),
@@ -387,8 +463,7 @@
             vm((3, taps, cb, full), F32),
             vm((3, 9 * cb, nz * cb2), BF16),
             vm((3, 9 * cb, nz * cb2), BF16),
-            vm((9 * cb, nz * cb2), BF16),
-            vm((2, 9 * cb, nz * hrows), BF16),
+            vm((3, 9 * cb, nz * hrows), BF16),
             vm((2, 9 * cb, cells), F32),
             vm((9 * cb, cells), F32),
             vm((3, 9 * cb, cells), F32),
@@ -397,18 +472,19 @@
             vm((n * piece, full), F32),
             *reduce_bufs,
             *reduce_bufs,
-            dma((nz,)), dma((nz,)), dma((2, nz)), dma((2, nz)),
+            dma((5,)), dma((5,)), dma((nz,)), dma((nz,)), dma((2, nz)), dma((2, nz)),
             dma((nz,)), dma((nz,)), dma((2,)), dma((2,)),
-            dma((nz,)), dma((nz,)), dma((2, nz)), dma((2, nz)),
+            dma((5,)), dma((nz,)), dma((nz,)), dma((5,)), dma((nz,)), dma((nz,)),
+            dma((2, nz)), dma((2, nz)),
             dma((n,)), dma((n,)), dma((n,)), dma((n,)),
             dma((n,)), dma((n,)), dma((n,)), dma((n,)),
         ],
         compiler_params=pltpu.CompilerParams(
             collective_id=0, has_side_effects=True, vmem_limit_bytes=48 << 20
         ),
-    )(block, mask.reshape(ys, -1), w_first, w_second)
+    )(feats, grads, mask, w_first, w_second)
     return (
-        gf.reshape(cb, 1, ys, zs),
+        gf,
         g1.reshape(taps, cb, full).transpose(0, 2, 1),
         g2.reshape(taps, cb, full).transpose(0, 2, 1),
     )

time: 45.9 us -> 50.5 us (1.10)
  Pallas kernels: 39.2 us -> 43 us
  local copies, waits for them, and re-layouts: 5.76 us -> 6.53 us
    pallas_call x1, Pallas kernels: 39.2 us -> 43 us  [body(): pl.pallas_call(functools.partial(kernel, n, nz, ys, zs, scale, 'space', '...]
    unnamed x9 -> x13, local copies, waits for them, and re-layouts: 4.92 us -> 6.53 us
    reshape x1 -> x0, local copies, waits for them, and re-layouts: 0.84 us -> none  [body(): grads.reshape(cb, cells)]
where the time goes in v2:
time: 50.5 us; the launch traced here: 50.1 us
  Pallas kernels  43 us (85%)
  local copies, waits for them, and re-layouts  6.53 us (13%)
  between operations  0.65 us (1%)
    pallas_call x1, Pallas kernels, body(): pl.pallas_call(functools.partial(kernel, n, nz, ys, zs, scale, 'space', '...  43 us
    unnamed x13, local copies, waits for them, and re-layouts  6.53 us

profile of v2, /device:TPU:0, one launch (start us, length us, event | category | flops | bytes accessed | tf_op | source)
XLA Modules:
  0.0 50.1 jit_solution(359079736937410271)
XLA Ops:
  0.6 0.0 copy-start
  0.6 1.1 %copy-done = bf16[27,96,96]{2,1,0:T(8,128)(2,1)S(1)} copy-done((bf16[27,96,96]{2,1,0:T(8,128)(2,1)S(1)}, bf16[27,96,96]{2,1,0:T(8,128)(2,1)}, u32[]{:S(2)}) %copy-start) | copy-done | bytes 497688
  1.7 0.0 copy-start.1
  1.7 1.1 %copy-done.1 = bf16[27,96,96]{2,1,0:T(8,128)(2,1)S(1)} copy-done((bf16[27,96,96]{2,1,0:T(8,128)(2,1)S(1)}, bf16[27,96,96]{2,1,0:T(8,128)(2,1)}, u32[]{:S(2)}) %copy-start.1) | copy-done | bytes 497688
  2.8 0.0 copy-start.2
  2.8 0.8 %copy-done.2 = bf16[24,1,8,128]{3,2,1,0:T(8,128)(2,1)S(1)} copy-done((bf16[24,1,8,128]{3,2,1,0:T(8,128)(2,1)S(1)}, bf16[24,1,8,128]{3,2,1,0:T(8,128)(2,1)}, u32[]{:S(2)}) %copy-start.2) | copy-done | bytes 49176
  3.6 0.0 copy-start.3
  3.6 0.8 %copy-done.3 = bf16[24,1,8,128]{3,2,1,0:T(8,128)(2,1)S(1)} copy-done((bf16[24,1,8,128]{3,2,1,0:T(8,128)(2,1)S(1)}, bf16[24,1,8,128]{3,2,1,0:T(8,128)(2,1)}, u32[]{:S(2)}) %copy-start.3) | copy-done | bytes 49176
  4.4 0.0 copy-start.4
  4.4 0.7 %copy-done.4 = s32[1,8,32]{2,1,0:T(8,128)S(1)} copy-done((s32[1,8,32]{2,1,0:T(8,128)S(1)}, s32[1,8,32]{2,1,0:T(8,128)}, u32[]{:S(2)}) %copy-start.4) | copy-done | bytes 1048
  5.1 43.0 %shard_map.76 = (bf16[24,1,8,128]{3,2,1,0:T(8,128)(2,1)S(1)}, f32[648,96]{1,0:T(8,128)S(1)}, f32[648,96]{1,0:T(8,128)S(1)}) custom-call(bf16[24,1,8,128]{3,2,1,0:T(8,128)(2,1)S(1)} %copy-done.2, bf16[24,1,8,128]{3,2,1,0:T(8,128)(2,1)S(1)} %copy-done.3, s32[1,8,32]{2,1,0:T(8,128)S(1)} %copy-done.4, bf16[27,96,96]{2,1,0:T(8,128)(2,1)S(1)} %copy-done, ...), custom_call_target="tpu_custom_call" | custom-call | tf_op jit(solution)/shard_map/pallas_call | solution.py:444
  48.1 0.6 %copy.11 = bf16[24,1,8,128]{3,2,1,0:T(8,128)(2,1)} copy(bf16[24,1,8,128]{3,2,1,0:T(8,128)(2,1)S(1)} %get-tuple-element.12) | data formatting | bytes 98304
  48.7 0.7 %copy.12 = f32[27,96,24]{1,2,0:T(8,128)} copy(f32[27,96,24]{1,2,0:T(8,128)S(1)} %bitcast.7) | data formatting | bytes 497664
  49.4 0.7 %copy.13 = f32[27,96,24]{1,2,0:T(8,128)} copy(f32[27,96,24]{1,2,0:T(8,128)S(1)} %bitcast.6) | data formatting | bytes 497664
Async XLA Ops:
  0.6 1.1 %copy-start = (bf16[27,96,96]{2,1,0:T(8,128)(2,1)S(1)}, bf16[27,96,96]{2,1,0:T(8,128)(2,1)}, u32[]{:S(2)}) copy-start(bf16[27,96,96]{2,1,0:T(8,128)(2,1)} %w1_hbm.1) | copy-start | bytes 1492996
  1.7 1.1 %copy-start.1 = (bf16[27,96,96]{2,1,0:T(8,128)(2,1)S(1)}, bf16[27,96,96]{2,1,0:T(8,128)(2,1)}, u32[]{:S(2)}) copy-start(bf16[27,96,96]{2,1,0:T(8,128)(2,1)} %w2_hbm.1) | copy-start | bytes 1492996
  2.8 0.8 %copy-start.2 = (bf16[24,1,8,128]{3,2,1,0:T(8,128)(2,1)S(1)}, bf16[24,1,8,128]{3,2,1,0:T(8,128)(2,1)}, u32[]{:S(2)}) copy-start(bf16[24,1,8,128]{3,2,1,0:T(8,128)(2,1)} %feats_hbm.1) | copy-start | bytes 147460
  3.6 0.8 %copy-start.3 = (bf16[24,1,8,128]{3,2,1,0:T(8,128)(2,1)S(1)}, bf16[24,1,8,128]{3,2,1,0:T(8,128)(2,1)}, u32[]{:S(2)}) copy-start(bf16[24,1,8,128]{3,2,1,0:T(8,128)(2,1)} %grads_hbm.1) | copy-start | bytes 147460
  4.4 0.7 %copy-start.4 = (s32[1,8,32]{2,1,0:T(8,128)S(1)}, s32[1,8,32]{2,1,0:T(8,128)}, u32[]{:S(2)}) copy-start(s32[1,8,32]{2,1,0:T(8,128)} %mask_hbm.1) | copy-start | bytes 3076

commit v3 on v1

--- a/solution.py
+++ b/solution.py
@@ -67,9 +67,9 @@
 
 def kernel(
     n, nz, ys, zs, scale, sp, ch_name,
-    block_ref, mask_ref, w1_ref, w2_ref,
+    block_ref, mask_ref, w1_hbm, w2_hbm,
     gf_ref, g1_ref, g2_ref,
-    B, MK, MX, M, W, WA, WB, WC, WH, PS, SH, SM, C, H, R32, R1, RR1, G1, R2, RR2, G2,
+    w1_ref, w2_ref, ws, B, MK, MX, M, W, WA, WB, WC, WH, PS, SH, SM, C, H, R32, R1, RR1, G1, R2, RR2, G2,
     zs1, zr1, hs1, hr1, ms1, mr1, mhs, mhr, zs2, zr2, hs2, hr2, s1, q1, s2, q2, t1, u1, t2, u2,
 ):
     s = lax.axis_index(sp)
@@ -87,6 +87,10 @@
             device_id=(ds, dc), device_id_type=MESH,
         )
 
+    load1 = pltpu.make_async_copy(w1_hbm, w1_ref, ws.at[0])
+    load2 = pltpu.make_async_copy(w2_hbm, w2_ref, ws.at[1])
+    load1.start()
+    load2.start()
     barrier = pltpu.get_barrier_semaphore()
 
     @pl.loop(1, nz)
@@ -126,6 +130,8 @@
 
     halo(me, True)
 
+    load1.wait()
+    load2.wait()
     pick = one_hot(cb, full, lambda r, q: q == r + cb * me)
 
     @pl.loop(0, 27)
@@ -377,9 +383,10 @@
             jax.ShapeDtypeStruct((rows, full), F32),
             jax.ShapeDtypeStruct((rows, full), F32),
         ),
-        in_specs=[spec] * 4,
+        in_specs=[spec] * 2 + [pl.BlockSpec(memory_space=pltpu.HBM)] * 2,
         out_specs=(spec,) * 3,
         scratch_shapes=[
+            vm((taps, full, full), BF16), vm((taps, full, full), BF16), dma((2,)),
             vm((3, nz, cb2, cells), BF16),
             vm((nz, ys, zs), F32),
             vm((3, ys, zs), F32),
@@ -406,7 +413,9 @@
         compiler_params=pltpu.CompilerParams(
             collective_id=0, has_side_effects=True, vmem_limit_bytes=48 << 20
         ),
-    )(block, mask.reshape(ys, -1), w_first, w_second)
+    )(block, mask.reshape(ys, -1),
+      pltpu.with_memory_space_constraint(w_first, pltpu.HBM),
+      pltpu.with_memory_space_constraint(w_second, pltpu.HBM))
     return (
         gf.reshape(cb, 1, ys, zs),
         g1.reshape(taps, cb, full).transpose(0, 2, 1),

time: 45.9 us -> 43.6 us (0.950)
  local copies, waits for them, and re-layouts: 5.76 us -> 3.58 us
    unnamed x9 -> x5, local copies, waits for them, and re-layouts: 4.92 us -> 2.74 us
where the time goes in v3:
time: 43.6 us; the launch traced here: 43.4 us
  Pallas kernels  39.2 us (90%)
  local copies, waits for them, and re-layouts  3.58 us (8%)
  between operations  0.66 us (2%)
    pallas_call x1, Pallas kernels, body(): pl.pallas_call(functools.partial(kernel, n, nz, ys, zs, scale, 'space', '...  39.2 us
    unnamed x5, local copies, waits for them, and re-layouts  2.74 us

profile of v3, /device:TPU:0, one launch (start us, length us, event | category | flops | bytes accessed | tf_op | source)
XLA Modules:
  0.0 43.4 jit_solution(1177000659280080635)
XLA Ops:
  0.6 0.8 %copy_bitcast_fusion = (bf16[24,1024]{1,0:T(8,128)(2,1)S(1)}, bf16[24,1024]{1,0:T(8,128)(2,1)S(1)}) fusion(bf16[3,8,8,128]{3,2,1,0:T(8,128)(2,1)} %bitcast.26, bf16[3,8,8,128]{3,2,1,0:T(8,128)(2,1)} %bitcast.27), kind=kLoop, calls=%fused_computation.1 | loop fusion | bytes 196608 | tf_op jit(solution)/shard_map/reshape | solution.py:371
  1.5 0.0 copy-start
  1.5 0.7 %copy-done = s32[1,8,32]{2,1,0:T(8,128)S(1)} copy-done((s32[1,8,32]{2,1,0:T(8,128)S(1)}, s32[1,8,32]{2,1,0:T(8,128)}, u32[]{:S(2)}) %copy-start) | copy-done | bytes 1048
  2.2 39.2 %shard_map.76 = (bf16[24,1024]{1,0:T(8,128)(2,1)S(1)}, f32[648,96]{1,0:T(8,128)S(1)}, f32[648,96]{1,0:T(8,128)S(1)}) custom-call(bf16[48,1024]{1,0:T(8,128)(2,1)S(1)} %pad_maximum_fusion.block_ref, s32[8,32]{1,0:T(8,128)S(1)} %bitcast.24, bf16[27,96,96]{2,1,0:T(8,128)(2,1)} %w1_hbm.1, bf16[27,96,96]{2,1,0:T(8,128)(2,1)} %w2_hbm.1), custom_call_target="tpu_custom_call" | custom-call | tf_op jit(solution)/shard_map/pallas_call | solution.py:379
  41.3 0.6 %copy.11 = bf16[3,8,8,128]{3,2,1,0:T(8,128)(2,1)} copy(bf16[3,8,8,128]{3,1,2,0:T(8,128)(2,1)S(1)} %bitcast.23) | data formatting | bytes 98304
  42.0 0.7 %copy.16 = f32[27,96,24]{1,2,0:T(8,128)} copy(f32[27,96,24]{1,2,0:T(8,128)S(1)} %bitcast.22) | data formatting | bytes 497664
  42.7 0.7 %copy.17 = f32[27,96,24]{1,2,0:T(8,128)} copy(f32[27,96,24]{1,2,0:T(8,128)S(1)} %bitcast.21) | data formatting | bytes 497664
  (1 shorter events, 0.0 us)
Async XLA Ops:
  1.5 0.7 %copy-start = (s32[1,8,32]{2,1,0:T(8,128)S(1)}, s32[1,8,32]{2,1,0:T(8,128)}, u32[]{:S(2)}) copy-start(s32[1,8,32]{2,1,0:T(8,128)} %param.7) | copy-start | bytes 3076
